TPU v7x, 256 devices: a whole 4x4x8 slice. The times are simulated.
256 devices in a mesh: dp: 8 (over z), label: 32 (over y, x, core).
Axes of the slice: x: 4, y: 4, z: 8, core: 2. Of those that a mesh axis runs over, the one named last changes fastest.
Arguments:
- enc: bfloat16 [262144, 768], P(('dp', 'label')), may hold values from -6 to 6
- proj: bfloat16 [768, 768], replicated, may hold values from -0.21875 to 0.21875
- head_weight: bfloat16 [4096, 768], P('label'), may hold values from -0.21875 to 0.21875
- shortlist: int32 [2048, 4], P(('dp', 'label')), may hold values from 0 to 31, all different within a row; in each aligned block of 8 rows (0 to 7, 8 to 15, ...) at most 2 rows name the same one
- positives: int32 [262144, 8], P(('dp', 'label')), may hold values from 0 to 511
- weight_num: int32 [4096], P('label'), may hold values from 1 to 16
- weight_den: int32 [4096], P('label'), may hold values from 1 to 16
Outputs:
- grad_enc: float32 [262144, 768], P(('dp', 'label'))
- grad_proj: float32 [768, 768], replicated
- grad_head: float32 [4096, 768], P('label', 'dp')
Inputs may be any that keep to these rules, and one draw needn't show every extreme that they name: `shortlist`: each row names 4 different clusters; among the rows of one device no cluster is named by more than 2 rows, and in every draw some cluster is named by exactly 2 rows of some device; every cluster is named somewhere.
All inputs are finite; a program needn't handle non-finite values.
Results may differ from a plain program's by a relative error of at most 0.005.
Values may be sent and summed in bfloat16 or wider, within the bound.
A program may use at most 128 MiB of HBM per device.

v0:
```python
import jax
import jax.numpy as jnp
from jax import lax
from jax.sharding import PartitionSpec as P


def contract(left, right, left_dim, right_dim):
    return lax.dot_general(
        left, right, (((left_dim,), (right_dim,)), ((), ())), preferred_element_type=jnp.float32
    )


def cluster_grads(hidden_rows, cluster_rows, cluster_scale, wanted, keeping):
    cluster_size = cluster_rows.shape[-2]
    sample_block = hidden_rows.shape[1]
    label_iota = jnp.arange(cluster_size, dtype=jnp.int32)
    logits = jnp.einsum(
        "msd,ld->msl", hidden_rows, cluster_rows, preferred_element_type=jnp.float32
    )
    target = jnp.zeros(logits.shape, jnp.bool_)
    for column in range(wanted.shape[2]):
        target = target | (wanted[:, :, column, None] == label_iota)
    scaled = cluster_scale * (jax.nn.sigmoid(logits) - target.astype(jnp.float32)) / sample_block
    grad_logits = (scaled * keeping[:, None, None]).astype(jnp.bfloat16)
    grad_part = jnp.einsum(
        "msl,ld->msd", grad_logits, cluster_rows, preferred_element_type=jnp.float32
    ).astype(jnp.bfloat16)
    grad_cluster = jnp.einsum(
        "msl,msd->ld", grad_logits, hidden_rows, preferred_element_type=jnp.float32
    )
    return (grad_part, grad_cluster)


def shards(enc, proj, head_weight, shortlist, positives, weight_num, weight_den):
    owners = lax.axis_size("label")
    block_count, beam_width = shortlist.shape
    samples, model_width = enc.shape
    sample_block = samples // block_count
    cluster_size = head_weight.shape[0]
    positive_count = positives.shape[1]
    pair_count = block_count * beam_width
    hidden = jnp.dot(enc, proj, preferred_element_type=jnp.float32).astype(jnp.bfloat16)
    hidden_blocks = hidden.reshape(block_count, sample_block, model_width)
    wanted_blocks = positives.reshape(block_count, sample_block, positive_count)
    capacity = max(2, 2 * pair_count // owners)
    slot_count = owners * capacity
    pair_owner = shortlist.reshape(pair_count)
    pair_iota = jnp.arange(pair_count, dtype=jnp.int32)
    earlier = (pair_owner[:, None] == pair_owner[None, :]) & (
        pair_iota[None, :] < pair_iota[:, None]
    )
    pair_rank = jnp.sum(earlier.astype(jnp.int32), axis=1)
    pair_slot = pair_owner * capacity + pair_rank
    slot_iota = jnp.arange(slot_count, dtype=jnp.int32)
    placed = pair_slot[None, :] == slot_iota[:, None]
    occupied = jnp.any(placed, axis=1).astype(jnp.int32)
    source_pair = jnp.sum(jnp.where(placed, pair_iota[None, :], 0), axis=1)
    source_block = source_pair // beam_width
    source_slot = source_pair % beam_width
    send_rows = jnp.take(hidden_blocks, source_block, axis=0)
    send_wanted = (
        jnp.take(wanted_blocks, source_block, axis=0) - (source_slot * cluster_size)[:, None, None]
    )
    recv_rows, recv_wanted, recv_occupied = (
        lax.all_to_all(send_rows, "label", split_axis=0, concat_axis=0, tiled=True),
        lax.all_to_all(send_wanted, "label", split_axis=0, concat_axis=0, tiled=True),
        lax.all_to_all(occupied, "label", split_axis=0, concat_axis=0, tiled=True),
    )
    cluster_scale = weight_num.astype(jnp.float32) / weight_den.astype(jnp.float32)
    grad_part, weight_part = cluster_grads(
        recv_rows, head_weight, cluster_scale, recv_wanted, recv_occupied.astype(jnp.float32)
    )
    returned = lax.all_to_all(grad_part, "label", split_axis=0, concat_axis=0, tiled=True)
    block_pick = jnp.sum(
        placed.reshape(slot_count, block_count, beam_width).astype(jnp.int32), axis=2
    ).T.astype(jnp.bfloat16)
    grad_hidden = jnp.einsum(
        "bm,msd->bsd", block_pick, returned, preferred_element_type=jnp.float32
    )
    grad_hidden = grad_hidden.reshape(samples, model_width).astype(jnp.bfloat16)
    grad_enc = contract(grad_hidden, proj, 1, 1)
    grad_proj = lax.psum(contract(enc, grad_hidden, 0, 0), ("dp", "label"))
    grad_head = lax.psum_scatter(weight_part, "dp", scatter_dimension=1, tiled=True)
    return (grad_enc, grad_proj, grad_head)


def solution(mesh):
    placed = (
        P(("dp", "label"), None),
        P(),
        P("label", None),
        P(("dp", "label"), None),
        P(("dp", "label"), None),
        P("label"),
        P("label"),
    )
    return jax.shard_map(
        shards,
        mesh=mesh,
        in_specs=placed,
        out_specs=(P(("dp", "label"), None), P(), P("label", "dp")),
        check_vma=False,
    )
```

profile of v0, /device:TPU:2, one launch (start us, length us, event | category | flops | bytes accessed | tf_op | source)
XLA Modules:
  0.0 717.9 jit_solution(10684612803308153281)
XLA Ops:
  8.0 0.0 copy-start
  8.0 0.9 copy.28
  8.9 0.1 eq.157
  9.0 0.2 convert_reduce_fusion.1
  9.2 0.1 fusion.15
  9.3 0.7 reshape.137
  10.0 7.6 %all-to-all-start.2 = ((s32[32,2,1]{1,2,0:T(1,128)}), s32[32,2,1]{1,2,0:T(1,128)S(1)}, u32[]{:S(2)}, u32[]{:S(2)}) async-start(s32[32,2,1]{1,2,0:T(1,128)} %bitcast.14), calls=%async_computation.2 | async-start | bytes 32768 | tf_op jit(solution)/shard_map/all_to_all | solution.py:67
  17.6 0.1 select_reduce_fusion
  17.8 1.4 gather_fusion.1
  19.1 0.0 copy-done
  19.1 2.7 convolution_convert_fusion.1
  21.8 0.9 select_subtract_fusion
  22.7 6.8 gather_fusion
  29.6 0.0 all-to-all-done.2
  29.6 7.5 %all-to-all-start.1 = ((s32[64,128,8]{1,2,0:T(8,128)}), s32[64,128,8]{1,2,0:T(8,128)S(1)}, u32[]{:S(2)}, u32[]{:S(2)}) async-start(s32[64,128,8]{1,2,0:T(8,128)} %select_subtract_fusion), calls=%async_computation.1 | async-start | bytes 524288 | tf_op jit(solution)/shard_map/all_to_all | solution.py:66
  37.1 10.9 %broadcast_select_fusion = bf16[64,128,768]{2,1,0:T(8,128)(2,1)} fusion(bf16[64,128,768]{2,1,0:T(8,128)(2,1)} %gather_fusion, pred[64]{0:T(512)(128)(4,1)S(1)} %compare_and_fusion), kind=kLoop, calls=%fused_computation.4 | loop fusion | flops 6291456 | bytes 25165888 | tf_op jit(solution)/shard_map/jit(_take)/select_n | solution.py:60
  48.0 0.0 copy-start.2
  48.0 0.0 copy-start.3
  48.0 0.0 copy-start.1
  48.0 0.0 all-to-all-done.1
  48.0 8.2 %all-to-all-start = ((bf16[64,128,768]{2,1,0:T(8,128)(2,1)}), bf16[64,128,768]{2,1,0:T(8,128)(2,1)}, u32[]{:S(2)}, u32[]{:S(2)}) async-start(bf16[64,128,768]{2,1,0:T(8,128)(2,1)} %broadcast_select_fusion), calls=%async_computation | async-start | bytes 25165824 | tf_op jit(solution)/shard_map/all_to_all | solution.py:65
  56.2 0.0 copy-done.2
  56.2 0.0 copy-done.3
  56.2 0.1 multiply_reduce_fusion
  56.3 0.1 mul.57
  56.4 0.2 fusion.21
  56.6 148.6 %all-to-all-done = bf16[64,128,768]{2,1,0:T(8,128)(2,1)} async-done(((bf16[64,128,768]{2,1,0:T(8,128)(2,1)}), bf16[64,128,768]{2,1,0:T(8,128)(2,1)}, u32[]{:S(2)}, u32[]{:S(2)}) %all-to-all-start) | async-done | bytes 12582944 | tf_op jit(solution)/shard_map/all_to_all | solution.py:65
  205.1 0.0 copy-done.1
  205.2 12.7 %multiply_convert_fusion = bf16[64,128,128]{2,1,0:T(8,128)(2,1)} fusion(bf16[64,128,768]{2,1,0:T(8,128)(2,1)} %all-to-all-done, f32[64]{0:T(128)S(1)} %mul.57, s32[64,128]{1,0:T(8,128)S(1)} %bitcast.50, s32[64,128]{1,0:T(8,128)S(1)} %bitcast.51, s32[64,128]{1,0:T(8,128)S(1)} %bitcast.52, s32[64,128]{1,0:T(8,128)S(1)} %bitcast.53, ...), kind=kOutput, calls=%fused_computation.6 | convolution fusion | flops 1634729984 | bytes 15139584 | tf_op jit(solution)/shard_map/msd,ld->msl/dot_general | solution.py:17
  217.8 6.3 convolution_convert_fusion
  224.2 22.9 %copy.33 = bf16[64,128,768]{2,1,0:T(8,128)(2,1)} copy(bf16[64,128,768]{2,0,1:T(8,128)(2,1)S(1)} %convolution_convert_fusion) | data formatting | bytes 25165824 | tf_op jit(solution)/shard_map/convert_element_type | solution.py:27
  247.1 16.4 %all-to-all-start.3 = ((bf16[64,128,768]{2,1,0:T(8,128)(2,1)}), bf16[64,128,768]{2,1,0:T(8,128)(2,1)}, u32[]{:S(2)}, u32[]{:S(2)}) async-start(bf16[64,128,768]{2,1,0:T(8,128)(2,1)} %copy.33), calls=%async_computation.3 | async-start | bytes 25165824 | tf_op jit(solution)/shard_map/all_to_all | solution.py:73
  263.5 0.2 all-reduce.2.cloned.1.call-start
  263.7 0.1 reduce_sum.32
  263.8 0.1 copy.30
  263.9 0.1 convert_reduce_fusion
  264.0 148.7 %all-to-all-done.3 = bf16[64,128,768]{2,1,0:T(8,128)(2,1)} async-done(((bf16[64,128,768]{2,1,0:T(8,128)(2,1)}), bf16[64,128,768]{2,1,0:T(8,128)(2,1)}, u32[]{:S(2)}, u32[]{:S(2)}) %all-to-all-start.3) | async-done | bytes 12582944 | tf_op jit(solution)/shard_map/all_to_all | solution.py:73
  412.7 18.0 %fusion.10 = bf16[8,128,768]{2,0,1:T(8,128)(2,1)S(1)} fusion(bf16[64,128,768]{2,1,0:T(8,128)(2,1)} %all-to-all-done.3, s32[64,8]{0,1:T(8,128)S(1)} %convert_reduce_fusion), kind=kOutput, calls=%fused_computation.24 | convolution fusion | flops 101450240 | bytes 14157824 | tf_op jit(solution)/shard_map/bm,msd->bsd/dot_general | solution.py:77
  430.7 0.3 copy.35
  431.0 2.8 convolution_bitcast_fusion
  433.8 0.0 all-reduce.2.cloned.1.call-update
  433.9 0.0 reduce-scatter.2.cloned.1.call-start
  433.9 10.9 %convolution_bitcast_fusion.1 = f32[128,768]{0,1:T(8,128)} fusion(bf16[64,128,128]{2,1,0:T(8,128)(2,1)} %multiply_convert_fusion, bf16[64,128,768]{2,1,0:T(8,128)(2,1)} %all-to-all-done), kind=kOutput, calls=%fused_computation.26 | convolution fusion | flops 1610612736 | bytes 15073280 | tf_op jit(solution)/shard_map/msl,msd->ld/dot_general | solution.py:28
  444.9 0.0 reduce-scatter.2.cloned.1.call-update
  444.9 4.4 fusion.22
  449.2 258.0 %all-reduce.2.cloned.1.call-done = f32[768,768]{0,1:T(8,128)} async-done(((f32[768,768]{0,1:T(8,128)}), f32[768,768]{0,1:T(8,128)}) %all-reduce.2.cloned.1.call-update) | async-done | bytes 2359312 | tf_op jit(solution)/shard_map/psum | solution.py:82
  707.2 3.0 copy.37
  710.2 0.0 reduce-scatter.2.cloned.1.call-done
  (8 shorter events, 0.1 us)
Async XLA Ops:
  8.0 11.1 %copy-start = (bf16[1024,768]{1,0:T(8,128)(2,1)S(1)}, bf16[1024,768]{1,0:T(8,128)(2,1)}, u32[]{:S(2)}) copy-start(bf16[1024,768]{1,0:T(8,128)(2,1)} %param.7) | copy-start | bytes 4718596
  10.0 19.6 %all-to-all-start.2 = ((s32[32,2,1]{1,2,0:T(1,128)}), s32[32,2,1]{1,2,0:T(1,128)S(1)}, u32[]{:S(2)}, u32[]{:S(2)}) async-start(s32[32,2,1]{1,2,0:T(1,128)} %bitcast.14), calls=%async_computation.2 | async-start | bytes 32768 | tf_op jit(solution)/shard_map/all_to_all | solution.py:67
  29.6 18.4 %all-to-all-start.1 = ((s32[64,128,8]{1,2,0:T(8,128)}), s32[64,128,8]{1,2,0:T(8,128)S(1)}, u32[]{:S(2)}, u32[]{:S(2)}) async-start(s32[64,128,8]{1,2,0:T(8,128)} %select_subtract_fusion), calls=%async_computation.1 | async-start | bytes 524288 | tf_op jit(solution)/shard_map/all_to_all | solution.py:66
  48.0 8.2 %copy-start.2 = (s32[128]{0:T(128)S(1)}, s32[128]{0:T(128)}, u32[]{:S(2)}) copy-start(s32[128]{0:T(128)} %param.13) | copy-start | bytes 1540
  48.0 8.2 %copy-start.3 = (s32[128]{0:T(128)S(1)}, s32[128]{0:T(128)}, u32[]{:S(2)}) copy-start(s32[128]{0:T(128)} %param.12) | copy-start | bytes 1540
  48.0 157.2 %copy-start.1 = (bf16[128,768]{1,0:T(8,128)(2,1)S(1)}, bf16[128,768]{1,0:T(8,128)(2,1)}, u32[]{:S(2)}) copy-start(bf16[128,768]{1,0:T(8,128)(2,1)} %param.9) | copy-start | bytes 589828
  48.0 157.2 %all-to-all-start = ((bf16[64,128,768]{2,1,0:T(8,128)(2,1)}), bf16[64,128,768]{2,1,0:T(8,128)(2,1)}, u32[]{:S(2)}, u32[]{:S(2)}) async-start(bf16[64,128,768]{2,1,0:T(8,128)(2,1)} %broadcast_select_fusion), calls=%async_computation | async-start | bytes 25165824 | tf_op jit(solution)/shard_map/all_to_all | solution.py:65
  247.1 165.6 %all-to-all-start.3 = ((bf16[64,128,768]{2,1,0:T(8,128)(2,1)}), bf16[64,128,768]{2,1,0:T(8,128)(2,1)}, u32[]{:S(2)}, u32[]{:S(2)}) async-start(bf16[64,128,768]{2,1,0:T(8,128)(2,1)} %copy.33), calls=%async_computation.3 | async-start | bytes 25165824 | tf_op jit(solution)/shard_map/all_to_all | solution.py:73
  263.5 443.7 %all-reduce.2.cloned.1.call-start = ((), (), s32[]{:S(2)}) async-start(), calls=%async_computation.5 | async-start | bytes 4718592 | tf_op jit(solution)/shard_map/psum | solution.py:82
  433.9 276.4 %reduce-scatter.2.cloned.1.call-start = ((), (), s32[]{:S(2)}) async-start(), calls=%async_computation.6 | async-start | bytes 442368 | tf_op jit(solution)/shard_map/reduce_scatter | solution.py:83
Sparse Core Ops, SparseCore 0:
  434.0 273.1 all-reduce.1
Sparse Core Ops, SparseCore 1:
  445.0 46.8 reduce-scatter.1
where the time goes:
time: 722 us; the launch traced here: 718 us
  waiting for transfers between devices  555 us (77%)
  matrix products  57.8 us (8%)
  starting transfers between devices  40 us (6%)
  local copies, waits for them, and re-layouts  36.6 us (5%)
  between operations  15.9 us (2%)
  other arithmetic  12.4 us (2%)
    psum x1, waiting for transfers between devices, shards(): grad_proj = lax.psum(contract(enc, grad_hidden, 0, 0), ('dp', 'label'))  258 us
    all_to_all x1, waiting for transfers between devices, shards(): lax.all_to_all(grad_part, 'label', split_axis=0, concat_axis=0, tiled=True)  149 us
    all_to_all x1, waiting for transfers between devices, shards(): lax.all_to_all(send_rows, 'label', split_axis=0, concat_axis=0, tiled=True)  149 us
    convert_element_type x1, local copies, waits for them, and re-layouts, cluster_grads(): grad_part = jnp.einsum('msl,ld->msd', grad_logits, cluster_rows, preferre...  22.9 us
    dot_general x1, matrix products, shards(): jnp.einsum('bm,msd->bsd', block_pick, returned, preferred_element_type=jn...  18 us
    all_to_all x1, starting transfers between devices, shards(): lax.all_to_all(grad_part, 'label', split_axis=0, concat_axis=0, tiled=True)  16.4 us
  transfers between devices with their start and end apart: 6, of which 3 were waited for; matrix products, arithmetic and copies ran while one was open for 6% of the time, Pallas kernels for 0%

commit v1 on v0

--- a/solution.py
+++ b/solution.py
@@ -2,6 +2,12 @@
 import jax.numpy as jnp
 from jax import lax
 from jax.sharding import PartitionSpec as P
+
+
+def rest_patch(panel, which_axis, across):
+    for k in (which_axis, across):
+        panel = lax.psum(panel, axis_name=k)
+    return panel
 
 
 def contract(left, right, left_dim, right_dim):
@@ -79,7 +85,7 @@
     )
     grad_hidden = grad_hidden.reshape(samples, model_width).astype(jnp.bfloat16)
     grad_enc = contract(grad_hidden, proj, 1, 1)
-    grad_proj = lax.psum(contract(enc, grad_hidden, 0, 0), ("dp", "label"))
+    grad_proj = rest_patch(contract(enc, grad_hidden, 0, 0), "label", "dp")
     grad_head = lax.psum_scatter(weight_part, "dp", scatter_dimension=1, tiled=True)
     return (grad_enc, grad_proj, grad_head)
 

time: 722 us -> 696 us (0.964)
  waiting for transfers between devices: 555 us -> 531 us
    psum x1 -> x2, waiting for transfers between devices: 258 us -> 197 us  [rest_patch(): panel = lax.psum(panel, axis_name=k)]
    reduce_scatter x1, waiting for transfers between devices: 0.01 us -> 36.2 us  [shards(): lax.psum_scatter(weight_part, 'dp', scatter_dimension=1, tiled=True)]
  transfers between devices with their start and end apart: 6 -> 7, of which waited for: 3 -> 5; matrix products, arithmetic and copies ran while one was open for 6% -> 6% of each run, Pallas kernels for 0% -> 0%
where the time goes in v1:
time: 696 us; the launch traced here: 692 us
  waiting for transfers between devices  531 us (76%)
  matrix products  57.8 us (8%)
  starting transfers between devices  40.1 us (6%)
  local copies, waits for them, and re-layouts  36.6 us (5%)
  between operations  14.1 us (2%)
  other arithmetic  12.4 us (2%)
    psum x2, waiting for transfers between devices, rest_patch(): panel = lax.psum(panel, axis_name=k)  197 us
    all_to_all x1, waiting for transfers between devices, shards(): lax.all_to_all(grad_part, 'label', split_axis=0, concat_axis=0, tiled=True)  149 us
    all_to_all x1, waiting for transfers between devices, shards(): lax.all_to_all(send_rows, 'label', split_axis=0, concat_axis=0, tiled=True)  149 us
    reduce_scatter x1, waiting for transfers between devices, shards(): lax.psum_scatter(weight_part, 'dp', scatter_dimension=1, tiled=True)  36.2 us
    convert_element_type x1, local copies, waits for them, and re-layouts, cluster_grads(): grad_part = jnp.einsum('msl,ld->msd', grad_logits, cluster_rows, preferre...  22.9 us
    dot_general x1, matrix products, shards(): jnp.einsum('bm,msd->bsd', block_pick, returned, preferred_element_type=jn...  18 us
    all_to_all x1, starting transfers between devices, shards(): lax.all_to_all(grad_part, 'label', split_axis=0, concat_axis=0, tiled=True)  16.4 us
  transfers between devices with their start and end apart: 7, of which 5 were waited for; matrix products, arithmetic and copies ran while one was open for 6% of the time, Pallas kernels for 0%

profile of v1, /device:TPU:2, one launch (start us, length us, event | category | flops | bytes accessed | tf_op | source)
XLA Modules:
  0.0 691.8 jit_solution(6839907165694888585)
XLA Ops:
  7.2 0.0 copy-start
  7.2 0.9 copy.28
  8.1 0.1 eq.157
  8.1 0.2 convert_reduce_fusion.1
  8.3 0.1 fusion.15
  8.4 0.7 reshape.137
  9.1 7.6 %all-to-all-start.2 = ((s32[32,2,1]{1,2,0:T(1,128)}), s32[32,2,1]{1,2,0:T(1,128)S(1)}, u32[]{:S(2)}, u32[]{:S(2)}) async-start(s32[32,2,1]{1,2,0:T(1,128)} %bitcast.14), calls=%async_computation.2 | async-start | bytes 32768 | tf_op jit(solution)/shard_map/all_to_all | solution.py:73
  16.8 0.1 select_reduce_fusion
  16.9 1.4 gather_fusion.1
  18.3 0.0 copy-done
  18.3 2.7 convolution_convert_fusion.1
  21.0 0.9 select_subtract_fusion
  21.9 6.8 gather_fusion
  28.7 0.0 all-to-all-done.2
  28.7 7.5 %all-to-all-start.1 = ((s32[64,128,8]{1,2,0:T(8,128)}), s32[64,128,8]{1,2,0:T(8,128)S(1)}, u32[]{:S(2)}, u32[]{:S(2)}) async-start(s32[64,128,8]{1,2,0:T(8,128)} %select_subtract_fusion), calls=%async_computation.1 | async-start | bytes 524288 | tf_op jit(solution)/shard_map/all_to_all | solution.py:72
  36.2 10.9 %broadcast_select_fusion = bf16[64,128,768]{2,1,0:T(8,128)(2,1)} fusion(bf16[64,128,768]{2,1,0:T(8,128)(2,1)} %gather_fusion, pred[64]{0:T(512)(128)(4,1)S(1)} %compare_and_fusion), kind=kLoop, calls=%fused_computation.4 | loop fusion | flops 6291456 | bytes 25165888 | tf_op jit(solution)/shard_map/jit(_take)/select_n | solution.py:66
  47.1 0.0 copy-start.2
  47.1 0.0 copy-start.3
  47.1 0.0 copy-start.1
  47.1 0.0 all-to-all-done.1
  47.1 8.2 %all-to-all-start = ((bf16[64,128,768]{2,1,0:T(8,128)(2,1)}), bf16[64,128,768]{2,1,0:T(8,128)(2,1)}, u32[]{:S(2)}, u32[]{:S(2)}) async-start(bf16[64,128,768]{2,1,0:T(8,128)(2,1)} %broadcast_select_fusion), calls=%async_computation | async-start | bytes 25165824 | tf_op jit(solution)/shard_map/all_to_all | solution.py:71
  55.4 0.0 copy-done.2
  55.4 0.0 copy-done.3
  55.4 0.1 multiply_reduce_fusion
  55.5 0.1 mul.57
  55.6 0.2 fusion.21
  55.8 148.6 %all-to-all-done = bf16[64,128,768]{2,1,0:T(8,128)(2,1)} async-done(((bf16[64,128,768]{2,1,0:T(8,128)(2,1)}), bf16[64,128,768]{2,1,0:T(8,128)(2,1)}, u32[]{:S(2)}, u32[]{:S(2)}) %all-to-all-start) | async-done | bytes 12582944 | tf_op jit(solution)/shard_map/all_to_all | solution.py:71
  204.3 0.0 copy-done.1
  204.3 12.7 %multiply_convert_fusion = bf16[64,128,128]{2,1,0:T(8,128)(2,1)} fusion(bf16[64,128,768]{2,1,0:T(8,128)(2,1)} %all-to-all-done, f32[64]{0:T(128)S(1)} %mul.57, s32[64,128]{1,0:T(8,128)S(1)} %bitcast.50, s32[64,128]{1,0:T(8,128)S(1)} %bitcast.51, s32[64,128]{1,0:T(8,128)S(1)} %bitcast.52, s32[64,128]{1,0:T(8,128)S(1)} %bitcast.53, ...), kind=kOutput, calls=%fused_computation.6 | convolution fusion | flops 1634729984 | bytes 15139584 | tf_op jit(solution)/shard_map/msd,ld->msl/dot_general | solution.py:23
  217.0 6.3 convolution_convert_fusion
  223.3 22.9 %copy.33 = bf16[64,128,768]{2,1,0:T(8,128)(2,1)} copy(bf16[64,128,768]{2,0,1:T(8,128)(2,1)S(1)} %convolution_convert_fusion) | data formatting | bytes 25165824 | tf_op jit(solution)/shard_map/convert_element_type | solution.py:33
  246.2 16.4 %all-to-all-start.3 = ((bf16[64,128,768]{2,1,0:T(8,128)(2,1)}), bf16[64,128,768]{2,1,0:T(8,128)(2,1)}, u32[]{:S(2)}, u32[]{:S(2)}) async-start(bf16[64,128,768]{2,1,0:T(8,128)(2,1)} %copy.33), calls=%async_computation.3 | async-start | bytes 25165824 | tf_op jit(solution)/shard_map/all_to_all | solution.py:79
  262.7 0.2 all-reduce.3.cloned.1.call-start
  262.9 0.1 reduce_sum.32
  263.0 0.1 copy.30
  263.1 0.1 convert_reduce_fusion
  263.1 148.7 %all-to-all-done.3 = bf16[64,128,768]{2,1,0:T(8,128)(2,1)} async-done(((bf16[64,128,768]{2,1,0:T(8,128)(2,1)}), bf16[64,128,768]{2,1,0:T(8,128)(2,1)}, u32[]{:S(2)}, u32[]{:S(2)}) %all-to-all-start.3) | async-done | bytes 12582944 | tf_op jit(solution)/shard_map/all_to_all | solution.py:79
  411.9 18.0 %fusion.10 = bf16[8,128,768]{2,0,1:T(8,128)(2,1)S(1)} fusion(bf16[64,128,768]{2,1,0:T(8,128)(2,1)} %all-to-all-done.3, s32[64,8]{0,1:T(8,128)S(1)} %convert_reduce_fusion), kind=kOutput, calls=%fused_computation.24 | convolution fusion | flops 101450240 | bytes 14157824 | tf_op jit(solution)/shard_map/bm,msd->bsd/dot_general | solution.py:83
  429.9 0.3 copy.35
  430.2 2.8 convolution_bitcast_fusion
  433.0 0.0 all-reduce.3.cloned.1.call-update
  433.0 0.0 all-reduce.5.cloned.1.call-start
  433.1 126.3 %all-reduce.3.cloned.1.call-done = f32[768,768]{0,1:T(8,128)} async-done(((f32[768,768]{0,1:T(8,128)}), f32[768,768]{0,1:T(8,128)}) %all-reduce.3.cloned.1.call-update) | async-done | bytes 2359312 | tf_op jit(solution)/shard_map/psum | solution.py:9
  559.3 0.0 all-reduce.5.cloned.1.call-update
  559.4 0.0 reduce-scatter.2.cloned.1.call-start
  559.4 11.0 %convolution_bitcast_fusion.1 = f32[128,768]{0,1:T(8,128)} fusion(bf16[64,128,128]{2,1,0:T(8,128)(2,1)} %multiply_convert_fusion, bf16[64,128,768]{2,1,0:T(8,128)(2,1)} %all-to-all-done), kind=kOutput, calls=%fused_computation.26 | convolution fusion | flops 1610612736 | bytes 15073280 | tf_op jit(solution)/shard_map/msl,msd->ld/dot_general | solution.py:34
  570.4 0.0 reduce-scatter.2.cloned.1.call-update
  570.4 4.4 fusion.22
  574.7 71.0 %all-reduce.5.cloned.1.call-done = f32[768,768]{0,1:T(8,128)} async-done(((f32[768,768]{0,1:T(8,128)}), f32[768,768]{0,1:T(8,128)}) %all-reduce.5.cloned.1.call-update) | async-done | bytes 2359312 | tf_op jit(solution)/shard_map/psum | solution.py:9
  645.8 3.0 copy.37
  648.8 36.2 %reduce-scatter.2.cloned.1.call-done = f32[128,96]{0,1:T(8,128)} async-done(((f32[128,768]{0,1:T(8,128)}), f32[128,96]{0,1:T(8,128)}) %reduce-scatter.2.cloned.1.call-update) | async-done | bytes 49168 | tf_op jit(solution)/shard_map/reduce_scatter | solution.py:89
  (8 shorter events, 0.1 us)
Async XLA Ops:
  7.2 11.1 %copy-start = (bf16[1024,768]{1,0:T(8,128)(2,1)S(1)}, bf16[1024,768]{1,0:T(8,128)(2,1)}, u32[]{:S(2)}) copy-start(bf16[1024,768]{1,0:T(8,128)(2,1)} %param.7) | copy-start | bytes 4718596
  9.1 19.6 %all-to-all-start.2 = ((s32[32,2,1]{1,2,0:T(1,128)}), s32[32,2,1]{1,2,0:T(1,128)S(1)}, u32[]{:S(2)}, u32[]{:S(2)}) async-start(s32[32,2,1]{1,2,0:T(1,128)} %bitcast.14), calls=%async_computation.2 | async-start | bytes 32768 | tf_op jit(solution)/shard_map/all_to_all | solution.py:73
  28.7 18.4 %all-to-all-start.1 = ((s32[64,128,8]{1,2,0:T(8,128)}), s32[64,128,8]{1,2,0:T(8,128)S(1)}, u32[]{:S(2)}, u32[]{:S(2)}) async-start(s32[64,128,8]{1,2,0:T(8,128)} %select_subtract_fusion), calls=%async_computation.1 | async-start | bytes 524288 | tf_op jit(solution)/shard_map/all_to_all | solution.py:72
  47.1 8.2 %copy-start.2 = (s32[128]{0:T(128)S(1)}, s32[128]{0:T(128)}, u32[]{:S(2)}) copy-start(s32[128]{0:T(128)} %param.13) | copy-start | bytes 1540
  47.1 8.2 %copy-start.3 = (s32[128]{0:T(128)S(1)}, s32[128]{0:T(128)}, u32[]{:S(2)}) copy-start(s32[128]{0:T(128)} %param.12) | copy-start | bytes 1540
  47.1 157.2 %copy-start.1 = (bf16[128,768]{1,0:T(8,128)(2,1)S(1)}, bf16[128,768]{1,0:T(8,128)(2,1)}, u32[]{:S(2)}) copy-start(bf16[128,768]{1,0:T(8,128)(2,1)} %param.9) | copy-start | bytes 589828
  47.1 157.2 %all-to-all-start = ((bf16[64,128,768]{2,1,0:T(8,128)(2,1)}), bf16[64,128,768]{2,1,0:T(8,128)(2,1)}, u32[]{:S(2)}, u32[]{:S(2)}) async-start(bf16[64,128,768]{2,1,0:T(8,128)(2,1)} %broadcast_select_fusion), calls=%async_computation | async-start | bytes 25165824 | tf_op jit(solution)/shard_map/all_to_all | solution.py:71
  246.2 165.6 %all-to-all-start.3 = ((bf16[64,128,768]{2,1,0:T(8,128)(2,1)}), bf16[64,128,768]{2,1,0:T(8,128)(2,1)}, u32[]{:S(2)}, u32[]{:S(2)}) async-start(bf16[64,128,768]{2,1,0:T(8,128)(2,1)} %copy.33), calls=%async_computation.3 | async-start | bytes 25165824 | tf_op jit(solution)/shard_map/all_to_all | solution.py:79
  262.7 296.7 %all-reduce.3.cloned.1.call-start = ((), (), s32[]{:S(2)}) async-start(), calls=%async_computation.5 | async-start | bytes 4718592 | tf_op jit(solution)/shard_map/psum | solution.py:9
  433.0 212.7 %all-reduce.5.cloned.1.call-start = ((), (), s32[]{:S(2)}) async-start(), calls=%async_computation.6 | async-start | bytes 4718592 | tf_op jit(solution)/shard_map/psum | solution.py:9
  559.4 125.7 %reduce-scatter.2.cloned.1.call-start = ((), (), s32[]{:S(2)}) async-start(), calls=%async_computation.7 | async-start | bytes 442368 | tf_op jit(solution)/shard_map/reduce_scatter | solution.py:89
Sparse Core Ops, SparseCore 0:
  433.2 126.1 all-reduce.2
  561.7 83.9 all-reduce.4
  648.9 36.1 reduce-scatter.1
